TPU v7x, 512 devices: a whole 4x4x16 slice. The times are simulated.
512 devices in a mesh: seq: 128 (over z, y, core), mp: 4 (over x).
Axes of the slice: x: 4, y: 4, z: 16, core: 2. Of those that a mesh axis runs over, the one named last changes fastest.
Arguments:
- queries: bfloat16 [8192, 2048], P('seq', 'mp'), may hold values from -14 to 14
- keys: bfloat16 [8192, 2048], P('seq', 'mp'), may hold values from -14 to 14
- values: bfloat16 [8192, 2048], P('seq', 'mp'), may hold values from -6 to 6
- stream: bfloat16 [8192, 2048], P('seq', 'mp'), may hold values from -6 to 6
- seg_lengths: int32 [64], replicated, may hold values from 1 to 256, 8192 in all
- gain: float32 [2048], replicated, may hold values from 0.5 to 1.5
- w_out: bfloat16 [2048, 2048], P('mp', 'seq'), may hold values from -0.125 to 0.125
- w_gate: bfloat16 [2048, 3072], P('seq', 'mp'), may hold values from -0.125 to 0.125
- w_up: bfloat16 [2048, 3072], P('seq', 'mp'), may hold values from -0.125 to 0.125
- w_down: bfloat16 [3072, 2048], P('mp', 'seq'), may hold values from -0.109375 to 0.109375
Outputs:
- mixed: bfloat16 [8192, 2048], P('seq', 'mp')
Inputs may be any that keep to these rules, and one draw needn't show every extreme that they name: `seg_lengths`: the segments of landmarks 0 to 63 follow one another and cover the document's 8192 tokens.
All inputs are finite; a program needn't handle non-finite values.
Results may differ from a plain program's by a relative error of at most 0.014.
Values may be sent and summed in bfloat16 or wider, within the bound.
No kernel may reach another device: no remote copies, remote signals or barrier semaphores. Data moves between devices by JAX's collectives and lax.ppermute only.
A program may use at most 64 MiB of HBM per device.

v0:
```python
import math
import jax
import jax.numpy as jnp
from jax import lax
from jax.sharding import PartitionSpec as P

PINV_ITERS = 6
HEAD = 128
HIGH_ACCURACY = lax.Precision.HIGHEST
EPS = 1e-05


def inverse_rounds(anchor_block):
    eye = jnp.eye(anchor_block.shape[-1], dtype=jnp.float32)
    col_most = jnp.max(jnp.sum(anchor_block, axis=1), axis=-1)
    row_most = jnp.max(jnp.sum(anchor_block, axis=2), axis=-1)
    approx = jnp.swapaxes(anchor_block, 1, 2) / (col_most * row_most)[:, None, None]
    for step in range(PINV_ITERS):
        prod = jnp.einsum("hij,hjk->hik", anchor_block, approx, precision=HIGH_ACCURACY)
        inner = 7.0 * eye - prod
        inner = 15.0 * eye - jnp.einsum("hij,hjk->hik", prod, inner, precision=HIGH_ACCURACY)
        inner = 13.0 * eye - jnp.einsum("hij,hjk->hik", prod, inner, precision=HIGH_ACCURACY)
        approx = 0.25 * jnp.einsum("hij,hjk->hik", approx, inner, precision=HIGH_ACCURACY)
    return approx


def on_device(queries, keys, values, stream, seg_lengths, gain, w_out, w_gate, w_up, w_down):
    tok = queries.shape[0]
    width = queries.shape[1]
    heads = width // HEAD
    marks = seg_lengths.shape[0]
    score_scale = 1.0 / math.sqrt(HEAD)
    ends = jnp.cumsum(seg_lengths)
    starts = ends - seg_lengths
    place = lax.axis_index("seq") * tok + jnp.arange(tok, dtype=jnp.int32)
    member = ((place[:, None] >= starts[None, :]) & (place[:, None] < ends[None, :])).astype(
        jnp.bfloat16
    )
    query_part = jnp.dot(member.T, queries, preferred_element_type=jnp.float32)
    key_part = jnp.dot(member.T, keys, preferred_element_type=jnp.float32)
    query_sum, key_sum = lax.psum((query_part, key_part), "seq")
    counts = seg_lengths.astype(jnp.float32)[:, None]
    query_anchors = (query_sum / counts).reshape(marks, heads, HEAD)
    key_anchors = (key_sum / counts).reshape(marks, heads, HEAD)
    query_slice = queries.astype(jnp.float32).reshape(tok, heads, HEAD)
    key_slice = keys.astype(jnp.float32).reshape(tok, heads, HEAD)
    value_slice = values.astype(jnp.float32).reshape(tok, heads, HEAD)
    nearby_scores = jax.nn.softmax(
        jnp.einsum("brc,xrc->rbx", query_slice, key_anchors, precision=HIGH_ACCURACY) * score_scale,
        axis=-1,
    )
    anchor_block = jax.nn.softmax(
        jnp.einsum("oqc,bqc->qob", query_anchors, key_anchors, precision=HIGH_ACCURACY)
        * score_scale,
        axis=-1,
    )
    distant_scores = (
        jnp.einsum("gvb,lvb->vgl", query_anchors, key_slice, precision=HIGH_ACCURACY) * score_scale
    )
    local_peak = jnp.max(distant_scores, axis=-1)
    peak = lax.pmax(local_peak, "seq")
    layer_weights = jnp.exp(distant_scores - peak[..., None])
    local_mass = jnp.sum(layer_weights, axis=-1)
    slice_sum = jnp.einsum("vqb,bvn->vqn", layer_weights, value_slice, precision=HIGH_ACCURACY)
    mass, weighted = lax.psum((local_mass, slice_sum), "seq")
    collected_rows = weighted / mass[..., None]
    token_mixer = jnp.einsum(
        "svy,syc->svc", inverse_rounds(anchor_block), collected_rows, precision=HIGH_ACCURACY
    )
    attn = (
        jnp.einsum("ljz,lzx->jlx", nearby_scores, token_mixer, precision=HIGH_ACCURACY)
        .reshape(tok, width)
        .astype(jnp.bfloat16)
    )
    full_out = lax.all_gather(w_out, "seq", axis=1, tiled=True)
    out_terms = jnp.dot(attn, full_out, preferred_element_type=jnp.float32)
    proj = lax.psum_scatter(
        out_terms.astype(jnp.bfloat16), "mp", scatter_dimension=1, tiled=True
    ).astype(jnp.float32)
    resid = (stream.astype(jnp.float32) + proj).astype(jnp.bfloat16)
    whole = lax.all_gather(resid, "mp", axis=1, tiled=True)
    whole32 = whole.astype(jnp.float32)
    meansq = jnp.mean(whole32 * whole32, axis=-1, keepdims=True)
    normed = (whole32 * lax.rsqrt(meansq + EPS) * gain[None, :]).astype(jnp.bfloat16)
    full_gate, full_up = (
        lax.all_gather(w_gate, "seq", axis=0, tiled=True),
        lax.all_gather(w_up, "seq", axis=0, tiled=True),
    )
    gate = jnp.dot(normed, full_gate, preferred_element_type=jnp.float32)
    upper = jnp.dot(normed, full_up, preferred_element_type=jnp.float32)
    hidden = (jax.nn.silu(gate) * upper).astype(jnp.bfloat16)
    full_down = lax.all_gather(w_down, "seq", axis=1, tiled=True)
    down_terms = jnp.dot(hidden, full_down, preferred_element_type=jnp.float32)
    ffn = lax.psum_scatter(
        down_terms.astype(jnp.bfloat16), "mp", scatter_dimension=1, tiled=True
    ).astype(jnp.float32)
    return (resid.astype(jnp.float32) + ffn).astype(jnp.bfloat16)


def solution(mesh):
    return jax.shard_map(
        on_device,
        mesh=mesh,
        in_specs=(
            P("seq", "mp"),
            P("seq", "mp"),
            P("seq", "mp"),
            P("seq", "mp"),
            P(),
            P(),
            P("mp", "seq"),
            P("seq", "mp"),
            P("seq", "mp"),
            P("mp", "seq"),
        ),
        out_specs=P("seq", "mp"),
        check_vma=False,
    )
```

profile of v0, /device:TPU:8, one launch (start us, length us, event | category | flops | bytes accessed | tf_op | source)
XLA Modules:
  0.0 1539.0 jit_solution(13063598890913038582)
XLA Ops:
  6.5 0.8 copy.40
  7.5 0.7 fusion.82
  8.3 1.8 fusion.60
  10.1 0.9 fusion.59
  11.0 323.3 %all-reduce.4.cloned.1.call-done = f32[64,512]{1,0:T(8,128)} async-done(((f32[64,512]{1,0:T(8,128)}), f32[64,512]{1,0:T(8,128)}) %all-reduce.4.cloned.1.call-update) | async-done | bytes 131088 | tf_op jit(solution)/shard_map/psum | solution.py:41
  334.4 1.2 fusion.83
  335.6 243.6 %pmax.7 = f32[4,64]{1,0:T(4,128)S(1)} all-reduce(f32[4,64]{1,0:T(4,128)S(1)} %get-tuple-element.11), channel_id=1, replica_groups=mesh['seq'=128,'mp'=4] {'seq'}, use_global_device_ids=true, to_apply=%region_10.11 | all-reduce | flops 256 | bytes 2048 | tf_op jit(solution)/shard_map/pmax | solution.py:61
  579.2 1.8 fusion.29
  581.1 0.7 all-gather.5.cloned.1.call-update
  581.9 246.9 %psum.31 = f32[4,64]{1,0:T(4,128)S(1)} all-reduce(f32[4,64]{1,0:T(4,128)S(1)} %fusion.28), channel_id=1, replica_groups=mesh['seq'=128,'mp'=4] {'seq'}, use_global_device_ids=true, to_apply=%region_13.14 | all-reduce | flops 256 | bytes 2048 | tf_op jit(solution)/shard_map/psum | solution.py:65
  828.7 78.3 %all-reduce.6.cloned.1.call-done = (f32[64,512]{1,0:T(8,128)}, f32[4,64,128]{2,1,0:T(8,128)}) async-done(((f32[64,512]{1,0:T(8,128)}, f32[4,64,128]{2,1,0:T(8,128)}), (f32[64,512]{1,0:T(8,128)}, f32[4,64,128]{2,1,0:T(8,128)})) %all-reduce.6.cloned.1.call-update) | async-done | bytes 262160 | tf_op jit(solution)/shard_map/psum | solution.py:41
  907.0 1.3 fusion.85
  908.4 1.4 fusion.84
  910.2 0.4 fusion.68
  912.9 0.4 fusion.75
  914.1 0.4 fusion.73
  915.3 0.4 fusion.71
  918.5 127.5 %all-gather.5.cloned.1.call-done = bf16[512,2048]{0,1:T(8,128)(2,1)} async-done(((bf16[512,16]{0,1:T(8,128)(2,1)}), bf16[512,2048]{0,1:T(8,128)(2,1)}) %all-gather.5.cloned.1.call-update) | async-done | bytes 2097168 | tf_op jit(solution)/shard_map/all_gather | solution.py:75
  1045.9 3.0 convolution_convert_fusion.1
  1049.1 0.5 all-gather.7.cloned.1.call-update
  1049.7 0.5 all-gather.11.cloned.1.call-update
  1050.2 0.7 all-gather.9.cloned.1.call-update
  1051.0 23.7 %reduce-scatter.3.cloned.1.call-done = bf16[64,512]{1,0:T(8,128)(2,1)} async-done(((bf16[64,2048]{1,0:T(8,128)(2,1)}), bf16[64,512]{1,0:T(8,128)(2,1)}) %reduce-scatter.3.cloned.1.call-update) | async-done | bytes 65552 | tf_op jit(solution)/shard_map/reduce_scatter | solution.py:77
  1074.6 0.9 add_convert_fusion.1
  1075.5 12.3 all_gather.16
  1087.9 130.2 %all-gather.7.cloned.1.call-done = bf16[2048,768]{1,0:T(8,128)(2,1)} async-done(((bf16[16,768]{1,0:T(8,128)(2,1)}), bf16[2048,768]{1,0:T(8,128)(2,1)}) %all-gather.7.cloned.1.call-update) | async-done | bytes 3145744 | tf_op jit(solution)/shard_map/all_gather | solution.py:86
  1218.1 2.6 fusion.36
  1220.7 138.2 %all-gather.11.cloned.1.call-done = bf16[768,2048]{0,1:T(8,128)(2,1)} async-done(((bf16[768,16]{0,1:T(8,128)(2,1)}), bf16[768,2048]{0,1:T(8,128)(2,1)}) %all-gather.11.cloned.1.call-update) | async-done | bytes 3145744 | tf_op jit(solution)/shard_map/all_gather | solution.py:92
  1358.9 140.9 %all-gather.9.cloned.1.call-done = bf16[2048,768]{1,0:T(8,128)(2,1)} async-done(((bf16[16,768]{1,0:T(8,128)(2,1)}), bf16[2048,768]{1,0:T(8,128)(2,1)}) %all-gather.9.cloned.1.call-update) | async-done | bytes 3145744 | tf_op jit(solution)/shard_map/all_gather | solution.py:87
  1499.8 5.3 convolution_convert_fusion
  1505.1 25.5 %reduce-scatter.5.cloned.1.call-done = bf16[64,512]{1,0:T(8,128)(2,1)} async-done(((bf16[64,2048]{1,0:T(8,128)(2,1)}), bf16[64,512]{1,0:T(8,128)(2,1)}) %reduce-scatter.5.cloned.1.call-update) | async-done | bytes 65552 | tf_op jit(solution)/shard_map/reduce_scatter | solution.py:94
  1530.6 1.5 add_convert_fusion
  (55 shorter events, 7.6 us)
Async XLA Ops:
  6.5 3.6 copy-start
  6.5 327.8 %all-reduce.4.cloned.1.call-start = ((), (), s32[]{:S(2)}) async-start(), calls=%async_computation.2 | async-start | bytes 262144 | tf_op jit(solution)/shard_map/psum | solution.py:41
  10.1 897.0 %all-reduce.6.cloned.1.call-start = ((), (), s32[]{:S(2)}) async-start(), calls=%async_computation.9 | async-start | bytes 524288 | tf_op jit(solution)/shard_map/psum | solution.py:41
  581.0 464.9 %all-gather.5.cloned.1.call-start = ((), (), s32[]{:S(2)}) async-start(), calls=%async_computation.3 | async-start | bytes 2113536 | tf_op jit(solution)/shard_map/all_gather | solution.py:75
  581.7 492.9 %reduce-scatter.3.cloned.1.call-start = ((), (), s32[]{:S(2)}) async-start(), calls=%async_computation.4 | async-start | bytes 327680 | tf_op jit(solution)/shard_map/reduce_scatter | solution.py:77
  913.6 4.2 copy-start.3
  916.0 158.7 %copy-start.1 = (bf16[64,512]{1,0:T(8,128)(2,1)S(1)}, bf16[64,512]{1,0:T(8,128)(2,1)}, u32[]{:S(2)}) copy-start(bf16[64,512]{1,0:T(8,128)(2,1)} %param.13) | copy-start | bytes 196612
  916.5 301.6 %copy-start.2 = (f32[2048]{0:T(1024)S(1)}, f32[2048]{0:T(1024)}, u32[]{:S(2)}) copy-start(f32[2048]{0:T(1024)} %param.15) | copy-start | bytes 24580
  1049.0 169.1 %all-gather.7.cloned.1.call-start = ((), (), s32[]{:S(2)}) async-start(), calls=%async_computation.5 | async-start | bytes 3170304 | tf_op jit(solution)/shard_map/all_gather | solution.py:86
  1049.6 309.3 %all-gather.11.cloned.1.call-start = ((), (), s32[]{:S(2)}) async-start(), calls=%async_computation.7 | async-start | bytes 3170304 | tf_op jit(solution)/shard_map/all_gather | solution.py:92
  1050.2 449.6 %all-gather.9.cloned.1.call-start = ((), (), s32[]{:S(2)}) async-start(), calls=%async_computation.6 | async-start | bytes 3170304 | tf_op jit(solution)/shard_map/all_gather | solution.py:87
  1050.9 479.7 %reduce-scatter.5.cloned.1.call-start = ((), (), s32[]{:S(2)}) async-start(), calls=%async_computation.8 | async-start | bytes 327680 | tf_op jit(solution)/shard_map/reduce_scatter | solution.py:94
Sparse Core Ops, SparseCore 0:
  10.8 323.5 all-reduce.3
  581.1 325.8 all-reduce.5
  910.2 135.7 all-gather.4
  1049.1 25.4 reduce-scatter.2
  1078.1 139.9 all-gather.6
  1221.6 137.2 all-gather.10
  1362.5 137.2 all-gather.8
  1505.2 25.3 reduce-scatter.4
where the time goes:
time: 1540 us
  waiting for transfers between devices  990 us (64%)
  blocking collectives  503 us (33%)
  matrix products  27.2 us (2%)
    psum x2, waiting for transfers between devices, on_device(): query_sum, key_sum = lax.psum((query_part, key_part), 'seq')  402 us
    psum x1, blocking collectives, on_device(): mass, weighted = lax.psum((local_mass, slice_sum), 'seq')  247 us
    pmax x1, blocking collectives, on_device(): peak = lax.pmax(local_peak, 'seq')  244 us
    all_gather x1, waiting for transfers between devices, on_device(): lax.all_gather(w_up, 'seq', axis=0, tiled=True)  141 us
    all_gather x1, waiting for transfers between devices, on_device(): full_down = lax.all_gather(w_down, 'seq', axis=1, tiled=True)  138 us
    all_gather x1, waiting for transfers between devices, on_device(): lax.all_gather(w_gate, 'seq', axis=0, tiled=True)  130 us
    all_gather x1, waiting for transfers between devices, on_device(): full_out = lax.all_gather(w_out, 'seq', axis=1, tiled=True)  127 us
  transfers between devices with their start and end apart: 8, of which 8 were waited for; matrix products, arithmetic and copies ran while one was open for 1% of the time, Pallas kernels for 0%

commit v1 on v0

--- a/solution.py
+++ b/solution.py
@@ -89,7 +89,12 @@
     gate = jnp.dot(normed, full_gate, preferred_element_type=jnp.float32)
     upper = jnp.dot(normed, full_up, preferred_element_type=jnp.float32)
     hidden = (jax.nn.silu(gate) * upper).astype(jnp.bfloat16)
-    full_down = lax.all_gather(w_down, "seq", axis=1, tiled=True)
+    full_down = jnp.concatenate(
+        lax.all_to_all(
+            jnp.stack([w_down for _ in range(lax.axis_size("seq"))], axis=0), "seq", 0, 0
+        ),
+        axis=1,
+    )
     down_terms = jnp.dot(hidden, full_down, preferred_element_type=jnp.float32)
     ffn = lax.psum_scatter(
         down_terms.astype(jnp.bfloat16), "mp", scatter_dimension=1, tiled=True

time: 1540 us -> 1420 us (0.922)
  waiting for transfers between devices: 990 us -> 855 us
    all_gather x1 -> x0, waiting for transfers between devices: 138 us -> none  [on_device(): full_down = lax.all_gather(w_down, 'seq', axis=1, tiled=True)]
    all_gather x1, waiting for transfers between devices: 130 us -> 152 us  [on_device(): lax.all_gather(w_gate, 'seq', axis=0, tiled=True)]
  transfers between devices with their start and end apart: 8 -> 8, of which waited for: 8 -> 7; matrix products, arithmetic and copies ran while one was open for 1% -> 1% of each run, Pallas kernels for 0% -> 0%
where the time goes in v1:
time: 1420 us
  waiting for transfers between devices  855 us (60%)
  blocking collectives  503 us (35%)
  matrix products  27 us (2%)
    psum x2, waiting for transfers between devices, on_device(): query_sum, key_sum = lax.psum((query_part, key_part), 'seq')  402 us
    psum x1, blocking collectives, on_device(): mass, weighted = lax.psum((local_mass, slice_sum), 'seq')  247 us
    pmax x1, blocking collectives, on_device(): peak = lax.pmax(local_peak, 'seq')  244 us
    all_gather x1, waiting for transfers between devices, on_device(): lax.all_gather(w_gate, 'seq', axis=0, tiled=True)  152 us
    all_gather x1, waiting for transfers between devices, on_device(): lax.all_gather(w_up, 'seq', axis=0, tiled=True)  136 us
    all_gather x1, waiting for transfers between devices, on_device(): full_out = lax.all_gather(w_out, 'seq', axis=1, tiled=True)  127 us
  transfers between devices with their start and end apart: 8, of which 7 were waited for; matrix products, arithmetic and copies ran while one was open for 1% of the time, Pallas kernels for 0%

profile of v1, /device:TPU:8, one launch (start us, length us, event | category | flops | bytes accessed | tf_op | source)
XLA Modules:
  0.0 1418.1 jit_solution(9470087091315285443)
XLA Ops:
  6.5 0.8 copy.41
  7.5 0.7 fusion.82
  8.3 1.8 fusion.60
  10.1 0.9 fusion.59
  11.0 323.3 %all-reduce.4.cloned.1.call-done = f32[64,512]{1,0:T(8,128)} async-done(((f32[64,512]{1,0:T(8,128)}), f32[64,512]{1,0:T(8,128)}) %all-reduce.4.cloned.1.call-update) | async-done | bytes 131088 | tf_op jit(solution)/shard_map/psum | solution.py:41
  334.4 1.2 fusion.83
  335.6 243.6 %pmax.7 = f32[4,64]{1,0:T(4,128)S(1)} all-reduce(f32[4,64]{1,0:T(4,128)S(1)} %get-tuple-element.11), channel_id=1, replica_groups=mesh['seq'=128,'mp'=4] {'seq'}, use_global_device_ids=true, to_apply=%region_10.11 | all-reduce | flops 256 | bytes 2048 | tf_op jit(solution)/shard_map/pmax | solution.py:61
  579.2 1.8 fusion.29
  581.1 0.7 all-gather.4.cloned.1.call-update
  581.9 246.9 %psum.31 = f32[4,64]{1,0:T(4,128)S(1)} all-reduce(f32[4,64]{1,0:T(4,128)S(1)} %fusion.28), channel_id=1, replica_groups=mesh['seq'=128,'mp'=4] {'seq'}, use_global_device_ids=true, to_apply=%region_13.14 | all-reduce | flops 256 | bytes 2048 | tf_op jit(solution)/shard_map/psum | solution.py:65
  828.7 78.3 %all-reduce.6.cloned.1.call-done = (f32[64,512]{1,0:T(8,128)}, f32[4,64,128]{2,1,0:T(8,128)}) async-done(((f32[64,512]{1,0:T(8,128)}, f32[4,64,128]{2,1,0:T(8,128)}), (f32[64,512]{1,0:T(8,128)}, f32[4,64,128]{2,1,0:T(8,128)})) %all-reduce.6.cloned.1.call-update) | async-done | bytes 262160 | tf_op jit(solution)/shard_map/psum | solution.py:41
  907.0 1.3 fusion.85
  908.4 1.4 fusion.84
  910.2 0.4 fusion.68
  911.5 0.4 fusion.77
  912.9 0.4 fusion.75
  915.3 0.4 fusion.71
  918.4 127.5 %all-gather.4.cloned.1.call-done = bf16[512,2048]{0,1:T(8,128)(2,1)} async-done(((bf16[512,16]{0,1:T(8,128)(2,1)}), bf16[512,2048]{0,1:T(8,128)(2,1)}) %all-gather.4.cloned.1.call-update) | async-done | bytes 2097168 | tf_op jit(solution)/shard_map/all_gather | solution.py:75
  1045.9 3.0 convolution_convert_fusion.1
  1049.1 0.5 all-gather.6.cloned.1.call-update
  1049.6 1.9 stack.2
  1051.5 12.6 all-to-all-start
  1064.1 0.5 all-gather.8.cloned.1.call-update
  1064.7 9.9 reduce-scatter.3.cloned.1.call-done
  1074.6 0.9 add_convert_fusion.1
  1075.5 12.3 all_gather.13
  1087.9 152.4 %all-gather.6.cloned.1.call-done = bf16[2048,768]{1,0:T(8,128)(2,1)} async-done(((bf16[16,768]{1,0:T(8,128)(2,1)}), bf16[2048,768]{1,0:T(8,128)(2,1)}) %all-gather.6.cloned.1.call-update) | async-done | bytes 3145744 | tf_op jit(solution)/shard_map/all_gather | solution.py:86
  1240.3 3.3 fusion.36
  1243.6 136.2 %all-gather.8.cloned.1.call-done = bf16[2048,768]{1,0:T(8,128)(2,1)} async-done(((bf16[16,768]{1,0:T(8,128)(2,1)}), bf16[2048,768]{1,0:T(8,128)(2,1)}) %all-gather.8.cloned.1.call-update) | async-done | bytes 3145744 | tf_op jit(solution)/shard_map/all_gather | solution.py:87
  1379.8 4.4 convolution_convert_fusion
  1384.2 25.5 %reduce-scatter.5.cloned.1.call-done = bf16[64,512]{1,0:T(8,128)(2,1)} async-done(((bf16[64,2048]{1,0:T(8,128)(2,1)}), bf16[64,512]{1,0:T(8,128)(2,1)}) %reduce-scatter.5.cloned.1.call-update) | async-done | bytes 65552 | tf_op jit(solution)/shard_map/reduce_scatter | solution.py:99
  1409.8 1.5 add_convert_fusion
  (57 shorter events, 7.6 us)
Async XLA Ops:
  6.5 3.6 copy-start
  6.5 327.8 %all-reduce.4.cloned.1.call-start = ((), (), s32[]{:S(2)}) async-start(), calls=%async_computation.3 | async-start | bytes 262144 | tf_op jit(solution)/shard_map/psum | solution.py:41
  10.1 897.0 %all-reduce.6.cloned.1.call-start = ((), (), s32[]{:S(2)}) async-start(), calls=%async_computation.9 | async-start | bytes 524288 | tf_op jit(solution)/shard_map/psum | solution.py:41
  581.0 464.9 %all-gather.4.cloned.1.call-start = ((), (), s32[]{:S(2)}) async-start(), calls=%async_computation.4 | async-start | bytes 2113536 | tf_op jit(solution)/shard_map/all_gather | solution.py:75
  581.7 492.9 %reduce-scatter.3.cloned.1.call-start = ((), (), s32[]{:S(2)}) async-start(), calls=%async_computation.5 | async-start | bytes 327680 | tf_op jit(solution)/shard_map/reduce_scatter | solution.py:77
  913.6 4.2 copy-start.4
  916.0 133.6 %copy-start.3 = (bf16[768,16]{0,1:T(8,128)(2,1)S(1)}, bf16[768,16]{0,1:T(8,128)(2,1)}, u32[]{:S(2)}) copy-start(bf16[768,16]{0,1:T(8,128)(2,1)} %param.19) | copy-start | bytes 73732
  1049.0 191.3 %all-gather.6.cloned.1.call-start = ((), (), s32[]{:S(2)}) async-start(), calls=%async_computation.6 | async-start | bytes 3170304 | tf_op jit(solution)/shard_map/all_gather | solution.py:86
  1051.5 23.1 %copy-start.1 = (bf16[64,512]{1,0:T(8,128)(2,1)S(1)}, bf16[64,512]{1,0:T(8,128)(2,1)}, u32[]{:S(2)}) copy-start(bf16[64,512]{1,0:T(8,128)(2,1)} %param.13) | copy-start | bytes 196612
  1051.5 188.8 %copy-start.2 = (f32[2048]{0:T(1024)S(1)}, f32[2048]{0:T(1024)}, u32[]{:S(2)}) copy-start(f32[2048]{0:T(1024)} %param.15) | copy-start | bytes 24580
  1051.5 328.3 %all-to-all-start = ((bf16[128,768,16]{1,2,0:T(8,128)(2,1)}), bf16[128,768,16]{1,2,0:T(8,128)(2,1)S(1)}, u32[]{:S(2)}, u32[]{:S(2)}) async-start(bf16[128,768,16]{1,2,0:T(8,128)(2,1)} %stack.2), calls=%async_computation.1 | async-start | bytes 6291456 | tf_op jit(solution)/shard_map/all_to_all | solution.py:93
  1064.1 315.7 %all-gather.8.cloned.1.call-start = ((), (), s32[]{:S(2)}) async-start(), calls=%async_computation.7 | async-start | bytes 3170304 | tf_op jit(solution)/shard_map/all_gather | solution.py:87
  1064.7 345.1 %reduce-scatter.5.cloned.1.call-start = ((), (), s32[]{:S(2)}) async-start(), calls=%async_computation.8 | async-start | bytes 327680 | tf_op jit(solution)/shard_map/reduce_scatter | solution.py:99
Sparse Core Ops, SparseCore 0:
  10.8 323.5 all-reduce.3
  581.1 325.8 all-reduce.5
  910.2 135.7 all-gather.3
  1049.1 25.4 reduce-scatter.2
  1078.1 162.1 all-gather.5
  1243.8 135.9 all-gather.7
  1384.4 25.3 reduce-scatter.4
